TPU v7x, 256 devices: a whole 4x4x8 slice. The times are simulated.
256 devices in a mesh: tm: 32 (over z, x), region: 8 (over y, core).
Axes of the slice: x: 4, y: 4, z: 8, core: 2. Of those that a mesh axis runs over, the one named last changes fastest.
Arguments:
- start_primal: float32 [2048, 8, 3200], P('tm', 'region'), may hold values from 0 to 10, as said below
- demand: float32 [2048, 8, 3200], P('tm', 'region'), may hold values from -30 to 30
- unit_cost: float32 [8, 3200], P('region'), may hold values from -5 to 5
- build_cost: float32 [8, 128], P('region', 'tm'), may hold values from 0.5 to 2
- start_capacity: float32 [8, 128], P('region', 'tm'), may hold values from 0 to 2
- net_weights: float32 [8, 25, 3, 128, 128], P('region'), may hold values from -0.3125 to 0.3125
- net_columns: int32 [8, 25, 3], P('region'), may hold values from 0 to 24
- line_weights: float32 [8, 4, 128, 128], P('region'), may hold values from -0.25 to 0.25
- line_source: int32 [8, 4], replicated, may hold values from 0 to 7
- generator_map: int32 [8, 128], P('region'), may hold values from 0 to 127
Outputs:
- primal_final: float32 [2048, 8, 3200], P('tm', 'region')
- dual_final: float32 [2048, 8, 3200], P('tm', 'region')
- capacity_final: float32 [8, 128], P('region', 'tm')
Inputs may be any that keep to these rules, and one draw needn't show every extreme that they name: `start_primal`: Nonnegative.
All inputs are finite; a program needn't handle non-finite values.
Results may differ from a plain program's by a relative error of at most 0.0003.
Values sent between devices are 32-bit elements; how exact they have to be, the bound alone decides.
A program may use at most 64 MiB of HBM per device.

v0:
```python
import math
import jax
import jax.numpy as jnp
from jax import lax
from jax.sharding import PartitionSpec as P

ITERS = 4
HIGHEST_PRECISION = lax.Precision.HIGHEST
STEP_SCALE = 0.2
EPSILON = 1e-06


def shifted(shard, axis, by):
    devices = lax.axis_size(axis)
    pairs = [(i, i + by) for i in range(devices) if 0 <= i + by < devices]
    return lax.ppermute(shard, axis, pairs)


def network_forward(blocks, weights, columns):
    hour_count = blocks.shape[0]
    picked = jnp.take(blocks, columns.reshape(-1), axis=1)
    flat_weights = weights.reshape(-1, weights.shape[2], weights.shape[3])
    product = jnp.einsum("hpk,pkl->hpl", picked, flat_weights, precision=HIGHEST_PRECISION)
    return product.reshape(hour_count, columns.shape[0], columns.shape[1], -1).sum(axis=2)


def network_adjoint(dual_rows, weights, columns):
    hour_count = dual_rows.shape[0]
    partial_value = jnp.einsum("hil,iskl->hisk", dual_rows, weights, precision=HIGHEST_PRECISION)
    block_count = columns.shape[0]
    placing = (columns.reshape(-1)[:, None] == jnp.arange(block_count)[None, :]).astype(jnp.float32)
    stacked = partial_value.reshape(hour_count, -1, partial_value.shape[3])
    return jnp.einsum("hpk,pc->hck", stacked, placing, precision=HIGHEST_PRECISION)


def body(
    start_primal,
    demand,
    unit_cost,
    build_cost,
    start_capacity,
    net_weights,
    net_columns,
    line_weights,
    line_source,
    generator_map,
):
    hour_count, _, row_width = start_primal.shape
    block_size = net_weights.shape[3]
    block_count = row_width // block_size
    tm_count = lax.axis_size("tm")
    region_count = lax.axis_size("region")
    own_region = lax.axis_index("region")
    weights = net_weights[0]
    columns = net_columns[0]
    line_mats = line_weights[0]
    unit_rows = unit_cost.reshape(block_count, block_size)
    invest_own = start_capacity.shape[1]
    invest_all = invest_own * tm_count
    couple = 1.0 / math.sqrt(hour_count * tm_count)
    primal_count = hour_count * tm_count * region_count * row_width + region_count * invest_all
    dual_count = hour_count * tm_count * region_count * row_width
    selector = (generator_map[0][:, None] == jnp.arange(invest_all)[None, :]).astype(jnp.float32)
    line_links = (line_source[:, :, None] == jnp.arange(region_count)[None, None, :]).astype(
        jnp.float32
    )
    own_sources = lax.dynamic_index_in_dim(line_links, own_region, 0, keepdims=False)
    free_column = (jnp.arange(block_count) == 3)[None, :, None]
    free_row = (jnp.arange(block_count) < 3)[None, :, None]
    primal = start_primal.reshape(hour_count, block_count, block_size)
    target = demand.reshape(hour_count, block_count, block_size)
    dual = jnp.zeros_like(primal)
    primal_weight = jnp.float32(1.0)
    capacity, build_rows = (
        lax.all_gather(start_capacity[0], "tm", axis=0, tiled=True),
        lax.all_gather(build_cost[0], "tm", axis=0, tiled=True),
    )
    for iteration in range(ITERS):
        primal_step = STEP_SCALE / primal_weight
        dual_step = STEP_SCALE * primal_weight
        adjoint = network_adjoint(dual, weights, columns)
        after = shifted(dual[0, 0], "tm", -1)
        following = jnp.concatenate([dual[1:, 0], after[None]], axis=0)
        partial_lines = jnp.einsum(
            "hl,jkl->jhk", dual[:, 1], line_mats, precision=HIGHEST_PRECISION
        )
        line_back = lax.psum_scatter(
            jnp.einsum("jq,jhk->qhk", own_sources, partial_lines, precision=HIGHEST_PRECISION),
            "region",
            scatter_dimension=0,
            tiled=True,
        )[0]
        adjoint = adjoint.at[:, 0].add(-following).at[:, 3].add(line_back)
        column_sums = jnp.sum(dual[:, 2], axis=0)
        capacity_part = couple * jnp.dot(column_sums, selector, precision=HIGHEST_PRECISION)
        moved = primal - primal_step * (unit_rows[None] - adjoint)
        new_primal = jnp.where(free_column, moved, jnp.maximum(moved, 0.0))
        capacity_grad = lax.psum(capacity_part, "tm")
        new_capacity = jnp.maximum(capacity - primal_step * (build_rows - capacity_grad), 0.0)
        capacity_bar = 2.0 * new_capacity - capacity
        capacity_change = lax.dynamic_slice_in_dim(
            new_capacity - capacity, lax.axis_index("tm") * invest_own, invest_own, 0
        )
        primal_bar = 2.0 * new_primal - primal
        primal_local = jnp.sum((new_primal - primal) ** 2) + jnp.sum(capacity_change**2)
        if iteration + 1 < ITERS:
            primal_total = lax.psum(primal_local, ("tm", "region"))
        applied = network_forward(primal_bar, weights, columns)
        before = shifted(primal_bar[-1, 0], "tm", 1)
        earlier = jnp.concatenate([before[None], primal_bar[:-1, 0]], axis=0)
        chosen_flows = jnp.einsum(
            "jr,rhk->jhk",
            own_sources,
            lax.all_gather(primal_bar[:, 3][None], "region", axis=0, tiled=True),
            precision=HIGHEST_PRECISION,
        )
        line_flow = jnp.einsum("jhk,jkl->hl", chosen_flows, line_mats, precision=HIGHEST_PRECISION)
        picked_capacity = jnp.dot(selector, capacity_bar, precision=HIGHEST_PRECISION)
        applied = (
            applied.at[:, 0]
            .add(-earlier)
            .at[:, 1]
            .add(line_flow)
            .at[:, 2]
            .add(couple * picked_capacity[None])
        )
        moved_dual = dual + dual_step * (target - applied)
        new_dual = jnp.where(free_row, moved_dual, jnp.maximum(moved_dual, 0.0))
        if iteration + 1 < ITERS:
            dual_local = jnp.sum((new_dual - dual) ** 2)
            dual_total = lax.psum(dual_local, ("tm", "region"))
            primal_weight = jnp.sqrt(
                primal_weight
                * jnp.sqrt(primal_total / primal_count + EPSILON)
                / jnp.sqrt(dual_total / dual_count + EPSILON)
            )
        primal, dual, capacity = (new_primal, new_dual, new_capacity)
    capacity_own = lax.dynamic_slice_in_dim(
        capacity, lax.axis_index("tm") * invest_own, invest_own, 0
    )
    return (
        primal.reshape(hour_count, 1, row_width),
        dual.reshape(hour_count, 1, row_width),
        capacity_own[None],
    )


def solution(mesh):
    in_specs = (
        P("tm", "region", None),
        P("tm", "region", None),
        P("region", None),
        P("region", "tm"),
        P("region", "tm"),
        P("region", None, None, None, None),
        P("region", None, None),
        P("region", None, None, None),
        P(),
        P("region", None),
    )
    out_specs = (P("tm", "region", None), P("tm", "region", None), P("region", "tm"))
    return jax.shard_map(body, mesh=mesh, in_specs=in_specs, out_specs=out_specs, check_vma=False)
```

profile of v0, /device:TPU:1, one launch (start us, length us, event | category | flops | bytes accessed | tf_op | source)
XLA Modules:
  0.0 858.2 jit_solution(13189949462657411320)
XLA Ops:
  12.9 9.0 %fusion.6 = f32[25,64,3,128]{3,1,2,0:T(8,128)S(1)} fusion(f32[1,25,3,128,128]{4,3,2,1,0:T(8,128)} %param.57), kind=kOutput, calls=%fused_computation.10 | convolution fusion | flops 943718400 | bytes 7372800 | tf_op jit(solution)/shard_map/hil,iskl->hisk/dot_general | solution.py:29
  22.0 2.4 fusion.14
  27.1 76.9 %all-reduce.6 = (f32[128]{0:T(128)S(1)}, f32[128]{0:T(128)S(1)}, f32[128]{0:T(128)S(1)}) all-reduce(f32[128]{0:T(128)S(1)} %bitcast_dynamic-update-slice_fusion.1, f32[128]{0:T(128)S(1)} %bitcast_dynamic-update-slice_fusion, f32[128]{0:T(128)S(1)} %fusion.51), channel_id=2, replica_groups=mesh['tm'=32,'region'=8] {'tm'}, use_global_device_ids=true, to_apply=%add.1 | all-reduce | flops 384 | bytes 3072 | tf_op jit(solution)/shard_map/all_gather | solution.py:75
  106.3 3.1 reduce.43
  113.3 28.2 %all-gather.2 = f32[512,1,128]{2,1,0:T(1,128)S(1)} all-gather(f32[64,1,128]{2,1,0:T(1,128)S(1)} %bitcast.385), channel_id=4, replica_groups=mesh['tm'=32,'region'=8] {'region'}, dimensions={0}, use_global_device_ids=true | all-gather | bytes 294912 | tf_op jit(solution)/shard_map/all_gather | solution.py:114
  143.6 7.9 fusion.22
  157.0 10.5 %fusion.4 = f32[25,64,3,128]{3,1,2,0:T(8,128)} fusion(f32[1,25,3,128,128]{4,3,2,1,0:T(8,128)} %param.57, f32[64,25,128]{2,0,1:T(8,128)S(1)} %get-tuple-element.281), kind=kOutput, calls=%fused_computation.8 | convolution fusion | flops 943718400 | bytes 8192000 | tf_op jit(solution)/shard_map/hil,iskl->hisk/dot_general | solution.py:29
  167.7 55.8 %psum.73 = f32[128]{0:T(128)S(1)} all-reduce(f32[128]{0:T(128)S(1)} %fusion.49), channel_id=1, replica_groups=mesh['tm'=32,'region'=8] {'tm'}, use_global_device_ids=true, to_apply=%region_11.13 | all-reduce | flops 128 | bytes 1024 | tf_op jit(solution)/shard_map/psum | solution.py:98
  223.5 89.7 %all-reduce.5 = (f32[]{:T(128)}, f32[]{:T(128)}) all-reduce(f32[]{:T(128)S(6)} %add.249, f32[]{:T(128)} %get-tuple-element.280), channel_id=1, replica_groups=mesh['tm'=32,'region'=8] {'tm','region'}, use_global_device_ids=true, to_apply=%region_4.5 | all-reduce | flops 2 | bytes 16 | tf_op jit(solution)/shard_map/psum | solution.py:107
  317.6 4.0 fusion.12
  325.8 22.6 %reduce-scatter.7.cloned.1.call-done = f32[1,64,128]{2,1,0:T(8,128)} async-done(((f32[8,64,128]{2,1,0:T(8,128)}), f32[1,64,128]{2,1,0:T(8,128)}) %reduce-scatter.7.cloned.1.call-update) | async-done | bytes 32784 | tf_op jit(solution)/shard_map/reduce_scatter | solution.py:87
  354.9 2.8 collective-permute-start.3
  357.8 16.1 %all-gather.3 = f32[512,1,128]{2,1,0:T(1,128)S(1)} all-gather(f32[64,1,128]{2,1,0:T(1,128)S(1)} %bitcast.383), channel_id=5, replica_groups=mesh['tm'=32,'region'=8] {'region'}, dimensions={0}, use_global_device_ids=true | all-gather | bytes 294912 | tf_op jit(solution)/shard_map/all_gather | solution.py:114
  373.9 7.9 fusion.20
  387.2 10.5 %fusion.2 = f32[25,64,3,128]{3,1,2,0:T(8,128)} fusion(f32[1,25,3,128,128]{4,3,2,1,0:T(8,128)} %param.57, f32[64,25,128]{2,0,1:T(8,128)S(1)} %get-tuple-element.275), kind=kOutput, calls=%fused_computation.6 | convolution fusion | flops 943718400 | bytes 8192000 | tf_op jit(solution)/shard_map/hil,iskl->hisk/dot_general | solution.py:29
  397.9 59.1 %psum.76 = f32[128]{0:T(128)S(1)} all-reduce(f32[128]{0:T(128)S(1)} %fusion.47), channel_id=1, replica_groups=mesh['tm'=32,'region'=8] {'tm'}, use_global_device_ids=true, to_apply=%region_20.22 | all-reduce | flops 128 | bytes 1024 | tf_op jit(solution)/shard_map/psum | solution.py:98
  457.0 86.0 %all-reduce.4 = (f32[]{:T(128)}, f32[]{:T(128)}) all-reduce(f32[]{:T(128)S(6)} %add.257, f32[]{:T(128)} %get-tuple-element.274), channel_id=1, replica_groups=mesh['tm'=32,'region'=8] {'tm','region'}, use_global_device_ids=true, to_apply=%region_13.15 | all-reduce | flops 2 | bytes 16 | tf_op jit(solution)/shard_map/psum | solution.py:107
  547.2 4.0 fusion.10
  555.4 23.9 %reduce-scatter.9.cloned.1.call-done = f32[1,64,128]{2,1,0:T(8,128)} async-done(((f32[8,64,128]{2,1,0:T(8,128)}), f32[1,64,128]{2,1,0:T(8,128)}) %reduce-scatter.9.cloned.1.call-update) | async-done | bytes 32784 | tf_op jit(solution)/shard_map/reduce_scatter | solution.py:87
  580.7 2.2 multiply_reduce_fusion.1
  585.1 2.8 collective-permute-start.5
  587.9 16.1 %all-gather.4 = f32[512,1,128]{2,1,0:T(1,128)S(1)} all-gather(f32[64,1,128]{2,1,0:T(1,128)S(1)} %bitcast.384), channel_id=6, replica_groups=mesh['tm'=32,'region'=8] {'region'}, dimensions={0}, use_global_device_ids=true | all-gather | bytes 294912 | tf_op jit(solution)/shard_map/all_gather | solution.py:114
  604.0 7.9 fusion.18
  618.5 10.5 %fusion = f32[25,64,3,128]{3,1,2,0:T(8,128)} fusion(f32[1,25,3,128,128]{4,3,2,1,0:T(8,128)} %param.57, f32[64,25,128]{2,0,1:T(8,128)S(1)} %get-tuple-element.271), kind=kOutput, calls=%fused_computation.4 | convolution fusion | flops 943718400 | bytes 8192000 | tf_op jit(solution)/shard_map/hil,iskl->hisk/dot_general | solution.py:29
  629.2 59.1 %psum.79 = f32[128]{0:T(128)S(1)} all-reduce(f32[128]{0:T(128)S(1)} %fusion.45), channel_id=1, replica_groups=mesh['tm'=32,'region'=8] {'tm'}, use_global_device_ids=true, to_apply=%region_29.31 | all-reduce | flops 128 | bytes 1024 | tf_op jit(solution)/shard_map/psum | solution.py:98
  688.3 86.0 %all-reduce.3 = (f32[]{:T(128)}, f32[]{:T(128)}) all-reduce(f32[]{:T(128)S(6)} %add.266, f32[]{:T(128)} %get-tuple-element.270), channel_id=1, replica_groups=mesh['tm'=32,'region'=8] {'tm','region'}, use_global_device_ids=true, to_apply=%region_22.24 | all-reduce | flops 2 | bytes 16 | tf_op jit(solution)/shard_map/psum | solution.py:107
  778.5 4.0 fusion.8
  786.6 24.2 %reduce-scatter.11.cloned.1.call-done = f32[1,64,128]{2,1,0:T(8,128)} async-done(((f32[8,64,128]{2,1,0:T(8,128)}), f32[1,64,128]{2,1,0:T(8,128)}) %reduce-scatter.11.cloned.1.call-update) | async-done | bytes 32784 | tf_op jit(solution)/shard_map/reduce_scatter | solution.py:87
  812.2 2.7 multiply_subtract_fusion
  817.0 2.8 collective-permute-start.7
  819.9 16.1 %all-gather.5 = f32[512,1,128]{2,1,0:T(1,128)S(1)} all-gather(f32[64,1,128]{2,1,0:T(1,128)S(1)} %bitcast.382), channel_id=7, replica_groups=mesh['tm'=32,'region'=8] {'region'}, dimensions={0}, use_global_device_ids=true | all-gather | bytes 294912 | tf_op jit(solution)/shard_map/all_gather | solution.py:114
  836.0 8.0 fusion.16
  (174 shorter events, 71.9 us)
Async XLA Ops:
  7.2 97.1 %copy-start = (f32[64,1,3200]{2,1,0:T(1,128)S(1)}, f32[64,1,3200]{2,1,0:T(1,128)}, u32[]{:S(2)}) copy-start(f32[64,1,3200]{2,1,0:T(1,128)} %param.53) | copy-start | bytes 2457604
  7.2 102.9 %reduce-scatter.5.cloned.1.call-start = ((), (), s32[]{:S(2)}) async-start(), calls=%async_computation.4 | async-start | bytes 294912 | tf_op jit(solution)/shard_map/reduce_scatter | solution.py:87
  7.2 102.8 %collective-permute-start = (f32[128]{0:T(128)S(1)}, f32[128]{0:T(128)S(1)}, u32[]{:S(2)}, u32[]{:S(2)}) collective-permute-start(f32[128]{0:T(128)S(1)} %broadcast.305), channel_id=1, source_target_pairs={{8,0},{16,8},{24,16},{32,24},{40,32},{48,40},{56,48},{64,56},{72,6... | collective-permute-start | bytes 1544 | tf_op jit(solution)/shard_map/ppermute | solution.py:16
  12.0 336.4 %reduce-scatter.7.cloned.1.call-start = ((), (), s32[]{:S(2)}) async-start(), calls=%async_computation.5 | async-start | bytes 294912 | tf_op jit(solution)/shard_map/reduce_scatter | solution.py:87
  24.4 1.0 copy-start.14
  24.4 1.3 copy-start.16
  24.4 2.5 copy-start.12
  24.4 2.6 copy-start.13
  24.4 79.8 %copy-start.11 = (f32[1,3200]{1,0:T(1,128)S(1)}, f32[1,3200]{1,0:T(1,128)}, u32[]{:S(2)}) copy-start(f32[1,3200]{1,0:T(1,128)} %param.54) | copy-start | bytes 38404
  112.0 43.3 %collective-permute-start.1 = (f32[128]{0:T(128)S(1)}, f32[128]{0:T(128)S(1)}, u32[]{:S(2)}, u32[]{:S(2)}) collective-permute-start(f32[128]{0:T(128)S(1)} %slice_bitcast_fusion.16), channel_id=1, source_target_pairs={{0,8},{8,16},{16,24},{24,32},{32,40},{40,48},{48,56},{56,64},{64,7... | collective-permute-start | bytes 1544 | tf_op jit(solution)/shard_map/ppermute | solution.py:16
  151.5 3.8 copy-start.2
  156.6 10.9 %copy-start.8 = (f32[64,25,128]{2,0,1:T(8,128)}, f32[64,25,128]{2,0,1:T(8,128)S(1)}, u32[]{:S(2)}) copy-start(f32[64,25,128]{2,0,1:T(8,128)S(1)} %get-tuple-element.281) | copy-start | bytes 2457604
  167.7 153.9 %copy-start.15 = (s32[1,128]{1,0:T(1,128)S(1)}, s32[1,128]{1,0:T(1,128)}, u32[]{:S(2)}) copy-start(s32[1,128]{1,0:T(1,128)} %param.61) | copy-start | bytes 1540
  314.6 10.5 %collective-permute-start.2 = (f32[128]{0:T(128)S(1)}, f32[128]{0:T(128)S(1)}, u32[]{:S(2)}, u32[]{:S(2)}) collective-permute-start(f32[128]{0:T(128)S(1)} %slice_bitcast_fusion.15), channel_id=1, source_target_pairs={{8,0},{16,8},{24,16},{32,24},{40,32},{48,40},{56,48},{64,56},{72,6... | collective-permute-start | bytes 1544 | tf_op jit(solution)/shard_map/ppermute | solution.py:16
  317.1 262.2 %reduce-scatter.9.cloned.1.call-start = ((), (), s32[]{:S(2)}) async-start(), calls=%async_computation.6 | async-start | bytes 294912 | tf_op jit(solution)/shard_map/reduce_scatter | solution.py:87
  351.9 0.9 copy-start.3
  354.9 30.4 %collective-permute-start.3 = (f32[128]{0:T(128)S(1)}, f32[128]{0:T(128)S(1)}, u32[]{:S(2)}, u32[]{:S(2)}) collective-permute-start(f32[128]{0:T(128)S(1)} %slice_bitcast_fusion.14), channel_id=1, source_target_pairs={{0,8},{8,16},{16,24},{24,32},{32,40},{40,48},{48,56},{56,64},{64,7... | collective-permute-start | bytes 1544 | tf_op jit(solution)/shard_map/ppermute | solution.py:16
  381.8 4.0 copy-start.9
  386.8 10.9 %copy-start.7 = (f32[64,25,128]{2,0,1:T(8,128)}, f32[64,25,128]{2,0,1:T(8,128)S(1)}, u32[]{:S(2)}) copy-start(f32[64,25,128]{2,0,1:T(8,128)S(1)} %get-tuple-element.275) | copy-start | bytes 2457604
  544.5 10.3 %collective-permute-start.4 = (f32[128]{0:T(128)S(1)}, f32[128]{0:T(128)S(1)}, u32[]{:S(2)}, u32[]{:S(2)}) collective-permute-start(f32[128]{0:T(128)S(1)} %slice_bitcast_fusion.13), channel_id=1, source_target_pairs={{8,0},{16,8},{24,16},{32,24},{40,32},{48,40},{56,48},{64,56},{72,6... | collective-permute-start | bytes 1544 | tf_op jit(solution)/shard_map/ppermute | solution.py:16
  547.0 263.9 %reduce-scatter.11.cloned.1.call-start = ((), (), s32[]{:S(2)}) async-start(), calls=%async_computation.7 | async-start | bytes 294912 | tf_op jit(solution)/shard_map/reduce_scatter | solution.py:87
  551.2 29.5 %copy-start.4 = (f32[64,25,128]{2,0,1:T(8,128)S(1)}, f32[64,25,128]{2,0,1:T(8,128)}, u32[]{:S(2)}) copy-start(f32[64,25,128]{2,0,1:T(8,128)} %copy-done.3) | copy-start | bytes 2457604
  585.1 30.5 %collective-permute-start.5 = (f32[128]{0:T(128)S(1)}, f32[128]{0:T(128)S(1)}, u32[]{:S(2)}, u32[]{:S(2)}) collective-permute-start(f32[128]{0:T(128)S(1)} %slice_bitcast_fusion.12), channel_id=1, source_target_pairs={{0,8},{8,16},{16,24},{24,32},{32,40},{40,48},{48,56},{56,64},{64,7... | collective-permute-start | bytes 1544 | tf_op jit(solution)/shard_map/ppermute | solution.py:16
  618.1 10.9 %copy-start.5 = (f32[64,25,128]{2,0,1:T(8,128)}, f32[64,25,128]{2,0,1:T(8,128)S(1)}, u32[]{:S(2)}) copy-start(f32[64,25,128]{2,0,1:T(8,128)S(1)} %get-tuple-element.271) | copy-start | bytes 2457604
  775.8 10.2 %collective-permute-start.6 = (f32[128]{0:T(128)S(1)}, f32[128]{0:T(128)S(1)}, u32[]{:S(2)}, u32[]{:S(2)}) collective-permute-start(f32[128]{0:T(128)S(1)} %slice_bitcast_fusion.11), channel_id=1, source_target_pairs={{8,0},{16,8},{24,16},{32,24},{40,32},{48,40},{56,48},{64,56},{72,6... | collective-permute-start | bytes 1544 | tf_op jit(solution)/shard_map/ppermute | solution.py:16
  817.0 31.6 %collective-permute-start.7 = (f32[128]{0:T(128)S(1)}, f32[128]{0:T(128)S(1)}, u32[]{:S(2)}, u32[]{:S(2)}) collective-permute-start(f32[128]{0:T(128)S(1)} %slice_bitcast_fusion.10), channel_id=1, source_target_pairs={{0,8},{8,16},{16,24},{24,32},{32,40},{40,48},{48,56},{56,64},{64,7... | collective-permute-start | bytes 1544 | tf_op jit(solution)/shard_map/ppermute | solution.py:16
  836.0 8.4 copy-start.10
  844.9 4.1 copy-start.6
  848.9 2.4 copy-start.1
Sparse Core Ops, SparseCore 0:
  12.1 36.2 reduce-scatter.4
  317.2 31.0 reduce-scatter.6
  547.1 32.1 reduce-scatter.8
  778.6 32.1 reduce-scatter.10
where the time goes:
time: 867 us; the launch traced here: 858 us
  blocking collectives  589 us (68%)
  matrix products  94.9 us (11%)
  waiting for transfers between devices  70.8 us (8%)
  other arithmetic  35 us (4%)
  local copies, waits for them, and re-layouts  28.8 us (3%)
  between operations  23.7 us (3%)
  starting transfers between devices  16 us (2%)
    psum x3, blocking collectives, body(): primal_total = lax.psum(primal_local, ('tm', 'region'))  262 us
    psum x3, blocking collectives, body(): capacity_grad = lax.psum(capacity_part, 'tm')  174 us
    all_gather x1, blocking collectives, body(): lax.all_gather(start_capacity[0], 'tm', axis=0, tiled=True)  76.9 us
    all_gather x4, blocking collectives, body(): lax.all_gather(primal_bar[:, 3][None], 'region', axis=0, tiled=True)  76.5 us
    reduce_scatter x4, waiting for transfers between devices, body(): lax.psum_scatter(jnp.einsum('jq,jhk->qhk', own_sources, partial_lines, pr...  70.7 us
    dot_general x4, matrix products, network_adjoint(): jnp.einsum('hil,iskl->hisk', dual_rows, weights, precision=HIGHEST_PRECIS...  40.4 us
    dot_general x4, matrix products, network_forward(): jnp.einsum('hpk,pkl->hpl', picked, flat_weights, precision=HIGHEST_PRECIS...  31.7 us
  transfers between devices with their start and end apart: 12, of which 3 were waited for; matrix products, arithmetic and copies ran while one was open for 11% of the time, Pallas kernels for 0%

commit v1 on v0

--- a/solution.py
+++ b/solution.py
@@ -111,7 +111,12 @@
         chosen_flows = jnp.einsum(
             "jr,rhk->jhk",
             own_sources,
-            lax.all_gather(primal_bar[:, 3][None], "region", axis=0, tiled=True),
+            jnp.concatenate(
+                lax.all_to_all(
+                    jnp.stack([primal_bar[:, 3][None]] * lax.axis_size("region")), "region", 0, 0
+                ),
+                axis=0,
+            ),
             precision=HIGHEST_PRECISION,
         )
         line_flow = jnp.einsum("jhk,jkl->hl", chosen_flows, line_mats, precision=HIGHEST_PRECISION)

time: 867 us -> 844 us (0.973)
  blocking collectives: 589 us -> 519 us
  starting transfers between devices: 16 us -> 55.5 us
    all_gather x4 -> x0, blocking collectives: 76.5 us -> none  [body(): lax.all_gather(primal_bar[:, 3][None], 'region', axis=0, tiled=True)]
    all_to_all x0 -> x4, starting transfers between devices: none -> 39.7 us  [body(): lax.all_to_all(jnp.stack([primal_bar[:, 3][None]] * lax.axis_size('region...]
  transfers between devices with their start and end apart: 12 -> 16, of which waited for: 3 -> 3; matrix products, arithmetic and copies ran while one was open for 11% -> 12% of each run, Pallas kernels for 0% -> 0%
where the time goes in v1:
time: 844 us; the launch traced here: 835 us
  blocking collectives  519 us (61%)
  matrix products  96.3 us (11%)
  waiting for transfers between devices  69.7 us (8%)
  starting transfers between devices  55.5 us (7%)
  other arithmetic  38.7 us (5%)
  local copies, waits for them, and re-layouts  31.8 us (4%)
  between operations  23.7 us (3%)
    psum x3, blocking collectives, body(): primal_total = lax.psum(primal_local, ('tm', 'region'))  269 us
    psum x3, blocking collectives, body(): capacity_grad = lax.psum(capacity_part, 'tm')  174 us
    all_gather x1, blocking collectives, body(): lax.all_gather(start_capacity[0], 'tm', axis=0, tiled=True)  76.4 us
    reduce_scatter x4, waiting for transfers between devices, body(): lax.psum_scatter(jnp.einsum('jq,jhk->qhk', own_sources, partial_lines, pr...  69.6 us
    dot_general x4, matrix products, network_adjoint(): jnp.einsum('hil,iskl->hisk', dual_rows, weights, precision=HIGHEST_PRECIS...  40.4 us
    all_to_all x4, starting transfers between devices, body(): lax.all_to_all(jnp.stack([primal_bar[:, 3][None]] * lax.axis_size('region...  39.7 us
    dot_general x4, matrix products, network_forward(): jnp.einsum('hpk,pkl->hpl', picked, flat_weights, precision=HIGHEST_PRECIS...  31.7 us
  transfers between devices with their start and end apart: 16, of which 3 were waited for; matrix products, arithmetic and copies ran while one was open for 12% of the time, Pallas kernels for 0%

profile of v1, /device:TPU:1, one launch (start us, length us, event | category | flops | bytes accessed | tf_op | source)
XLA Modules:
  0.0 834.7 jit_solution(5229903335786133426)
XLA Ops:
  12.9 9.0 %fusion.6 = f32[25,64,3,128]{3,1,2,0:T(8,128)S(1)} fusion(f32[1,25,3,128,128]{4,3,2,1,0:T(8,128)} %param.57), kind=kOutput, calls=%fused_computation.10 | convolution fusion | flops 943718400 | bytes 7372800 | tf_op jit(solution)/shard_map/hil,iskl->hisk/dot_general | solution.py:29
  21.9 2.4 fusion.14
  27.1 76.4 %all-reduce.6 = (f32[128]{0:T(128)S(1)}, f32[128]{0:T(128)S(1)}, f32[128]{0:T(128)S(1)}) all-reduce(f32[128]{0:T(128)S(1)} %bitcast_dynamic-update-slice_fusion.1, f32[128]{0:T(128)S(1)} %bitcast_dynamic-update-slice_fusion, f32[128]{0:T(128)S(1)} %fusion.51), channel_id=2, replica_groups=mesh['tm'=32,'region'=8] {'tm'}, use_global_device_ids=true, to_apply=%add.1 | all-reduce | flops 384 | bytes 3072 | tf_op jit(solution)/shard_map/all_gather | solution.py:75
  105.8 3.1 reduce.43
  113.5 19.5 %all-to-all-start = ((f32[8,1,64,128]{3,2,1,0:T(8,128)}), f32[8,1,64,128]{3,2,1,0:T(8,128)S(1)}, u32[]{:S(2)}, u32[]{:S(2)}) async-start(f32[8,1,64,128]{3,2,1,0:T(8,128)} %stack.12), calls=%async_computation.1 | async-start | bytes 524288 | tf_op jit(solution)/shard_map/all_to_all | solution.py:115
  135.1 7.9 fusion.22
  148.6 10.5 %fusion.4 = f32[25,64,3,128]{3,1,2,0:T(8,128)} fusion(f32[1,25,3,128,128]{4,3,2,1,0:T(8,128)} %param.57, f32[64,25,128]{2,0,1:T(8,128)S(1)} %get-tuple-element.281), kind=kOutput, calls=%fused_computation.8 | convolution fusion | flops 943718400 | bytes 8192000 | tf_op jit(solution)/shard_map/hil,iskl->hisk/dot_general | solution.py:29
  159.3 55.7 %psum.73 = f32[128]{0:T(128)S(1)} all-reduce(f32[128]{0:T(128)S(1)} %fusion.49), channel_id=1, replica_groups=mesh['tm'=32,'region'=8] {'tm'}, use_global_device_ids=true, to_apply=%region_11.13 | all-reduce | flops 128 | bytes 1024 | tf_op jit(solution)/shard_map/psum | solution.py:98
  215.0 90.3 %all-reduce.5 = (f32[]{:T(128)}, f32[]{:T(128)}) all-reduce(f32[]{:T(128)S(6)} %add.249, f32[]{:T(128)} %get-tuple-element.280), channel_id=1, replica_groups=mesh['tm'=32,'region'=8] {'tm','region'}, use_global_device_ids=true, to_apply=%region_4.5 | all-reduce | flops 2 | bytes 16 | tf_op jit(solution)/shard_map/psum | solution.py:107
  309.6 4.0 fusion.12
  317.9 23.1 %reduce-scatter.7.cloned.1.call-done = f32[1,64,128]{2,1,0:T(8,128)} async-done(((f32[8,64,128]{2,1,0:T(8,128)}), f32[1,64,128]{2,1,0:T(8,128)}) %reduce-scatter.7.cloned.1.call-update) | async-done | bytes 32784 | tf_op jit(solution)/shard_map/reduce_scatter | solution.py:87
  347.6 2.8 collective-permute-start.3
  351.1 6.8 all-to-all-start.1
  357.9 7.9 fusion.20
  371.4 10.5 %fusion.2 = f32[25,64,3,128]{3,1,2,0:T(8,128)} fusion(f32[1,25,3,128,128]{4,3,2,1,0:T(8,128)} %param.57, f32[64,25,128]{2,0,1:T(8,128)S(1)} %get-tuple-element.275), kind=kOutput, calls=%fused_computation.6 | convolution fusion | flops 943718400 | bytes 8192000 | tf_op jit(solution)/shard_map/hil,iskl->hisk/dot_general | solution.py:29
  382.1 59.1 %psum.76 = f32[128]{0:T(128)S(1)} all-reduce(f32[128]{0:T(128)S(1)} %fusion.47), channel_id=1, replica_groups=mesh['tm'=32,'region'=8] {'tm'}, use_global_device_ids=true, to_apply=%region_20.22 | all-reduce | flops 128 | bytes 1024 | tf_op jit(solution)/shard_map/psum | solution.py:98
  441.2 89.2 %all-reduce.4 = (f32[]{:T(128)}, f32[]{:T(128)}) all-reduce(f32[]{:T(128)S(6)} %add.257, f32[]{:T(128)} %get-tuple-element.274), channel_id=1, replica_groups=mesh['tm'=32,'region'=8] {'tm','region'}, use_global_device_ids=true, to_apply=%region_13.15 | all-reduce | flops 2 | bytes 16 | tf_op jit(solution)/shard_map/psum | solution.py:107
  534.5 4.0 fusion.10
  542.7 23.2 %reduce-scatter.9.cloned.1.call-done = f32[1,64,128]{2,1,0:T(8,128)} async-done(((f32[8,64,128]{2,1,0:T(8,128)}), f32[1,64,128]{2,1,0:T(8,128)}) %reduce-scatter.9.cloned.1.call-update) | async-done | bytes 32784 | tf_op jit(solution)/shard_map/reduce_scatter | solution.py:87
  571.7 2.8 collective-permute-start.5
  575.2 6.7 all-to-all-start.2
  582.0 7.9 fusion.18
  591.2 2.9 reduce_sum.160
  601.5 10.5 %fusion = f32[25,64,3,128]{3,1,2,0:T(8,128)} fusion(f32[1,25,3,128,128]{4,3,2,1,0:T(8,128)} %param.57, f32[64,25,128]{2,0,1:T(8,128)S(1)} %get-tuple-element.271), kind=kOutput, calls=%fused_computation.4 | convolution fusion | flops 943718400 | bytes 8192000 | tf_op jit(solution)/shard_map/hil,iskl->hisk/dot_general | solution.py:29
  612.2 59.1 %psum.79 = f32[128]{0:T(128)S(1)} all-reduce(f32[128]{0:T(128)S(1)} %fusion.45), channel_id=1, replica_groups=mesh['tm'=32,'region'=8] {'tm'}, use_global_device_ids=true, to_apply=%region_29.31 | all-reduce | flops 128 | bytes 1024 | tf_op jit(solution)/shard_map/psum | solution.py:98
  671.3 89.2 %all-reduce.3 = (f32[]{:T(128)}, f32[]{:T(128)}) all-reduce(f32[]{:T(128)S(6)} %add.266, f32[]{:T(128)} %get-tuple-element.270), channel_id=1, replica_groups=mesh['tm'=32,'region'=8] {'tm','region'}, use_global_device_ids=true, to_apply=%region_22.24 | all-reduce | flops 2 | bytes 16 | tf_op jit(solution)/shard_map/psum | solution.py:107
  764.6 4.0 fusion.8
  772.8 23.3 %reduce-scatter.11.cloned.1.call-done = f32[1,64,128]{2,1,0:T(8,128)} async-done(((f32[8,64,128]{2,1,0:T(8,128)}), f32[1,64,128]{2,1,0:T(8,128)}) %reduce-scatter.11.cloned.1.call-update) | async-done | bytes 32784 | tf_op jit(solution)/shard_map/reduce_scatter | solution.py:87
  797.4 2.7 multiply_subtract_fusion
  802.3 2.8 collective-permute-start.7
  805.8 6.7 all-to-all-start.3
  812.5 8.0 fusion.16
  (184 shorter events, 79.1 us)
Async XLA Ops:
  7.2 96.6 %copy-start = (f32[64,1,3200]{2,1,0:T(1,128)S(1)}, f32[64,1,3200]{2,1,0:T(1,128)}, u32[]{:S(2)}) copy-start(f32[64,1,3200]{2,1,0:T(1,128)} %param.53) | copy-start | bytes 2457604
  7.2 102.4 %reduce-scatter.5.cloned.1.call-start = ((), (), s32[]{:S(2)}) async-start(), calls=%async_computation.8 | async-start | bytes 294912 | tf_op jit(solution)/shard_map/reduce_scatter | solution.py:87
  7.2 102.3 %collective-permute-start = (f32[128]{0:T(128)S(1)}, f32[128]{0:T(128)S(1)}, u32[]{:S(2)}, u32[]{:S(2)}) collective-permute-start(f32[128]{0:T(128)S(1)} %broadcast.313), channel_id=1, source_target_pairs={{8,0},{16,8},{24,16},{32,24},{40,32},{48,40},{56,48},{64,56},{72,6... | collective-permute-start | bytes 1544 | tf_op jit(solution)/shard_map/ppermute | solution.py:16
  24.3 1.3 copy-start.17
  24.4 2.5 copy-start.13
  24.4 2.6 copy-start.14
  24.4 79.3 %copy-start.12 = (f32[1,3200]{1,0:T(1,128)S(1)}, f32[1,3200]{1,0:T(1,128)}, u32[]{:S(2)}) copy-start(f32[1,3200]{1,0:T(1,128)} %param.54) | copy-start | bytes 38404
  111.5 34.9 %collective-permute-start.1 = (f32[128]{0:T(128)S(1)}, f32[128]{0:T(128)S(1)}, u32[]{:S(2)}, u32[]{:S(2)}) collective-permute-start(f32[128]{0:T(128)S(1)} %slice_bitcast_fusion.20), channel_id=1, source_target_pairs={{0,8},{8,16},{16,24},{24,32},{32,40},{40,48},{48,56},{56,64},{64,7... | collective-permute-start | bytes 1544 | tf_op jit(solution)/shard_map/ppermute | solution.py:16
  113.5 32.9 %all-to-all-start = ((f32[8,1,64,128]{3,2,1,0:T(8,128)}), f32[8,1,64,128]{3,2,1,0:T(8,128)S(1)}, u32[]{:S(2)}, u32[]{:S(2)}) async-start(f32[8,1,64,128]{3,2,1,0:T(8,128)} %stack.12), calls=%async_computation.1 | async-start | bytes 524288 | tf_op jit(solution)/shard_map/all_to_all | solution.py:115
  133.0 208.0 %reduce-scatter.7.cloned.1.call-start = ((), (), s32[]{:S(2)}) async-start(), calls=%async_computation.9 | async-start | bytes 294912 | tf_op jit(solution)/shard_map/reduce_scatter | solution.py:87
  143.0 3.8 copy-start.2
  148.2 10.9 %copy-start.9 = (f32[64,25,128]{2,0,1:T(8,128)}, f32[64,25,128]{2,0,1:T(8,128)S(1)}, u32[]{:S(2)}) copy-start(f32[64,25,128]{2,0,1:T(8,128)S(1)} %get-tuple-element.281) | copy-start | bytes 2457604
  159.3 154.4 %copy-start.16 = (s32[1,128]{1,0:T(1,128)S(1)}, s32[1,128]{1,0:T(1,128)}, u32[]{:S(2)}) copy-start(s32[1,128]{1,0:T(1,128)} %param.61) | copy-start | bytes 1540
  306.7 10.6 %collective-permute-start.2 = (f32[128]{0:T(128)S(1)}, f32[128]{0:T(128)S(1)}, u32[]{:S(2)}, u32[]{:S(2)}) collective-permute-start(f32[128]{0:T(128)S(1)} %slice_bitcast_fusion.19), channel_id=1, source_target_pairs={{8,0},{16,8},{24,16},{32,24},{40,32},{48,40},{56,48},{64,56},{72,6... | collective-permute-start | bytes 1544 | tf_op jit(solution)/shard_map/ppermute | solution.py:16
  347.6 21.6 %collective-permute-start.3 = (f32[128]{0:T(128)S(1)}, f32[128]{0:T(128)S(1)}, u32[]{:S(2)}, u32[]{:S(2)}) collective-permute-start(f32[128]{0:T(128)S(1)} %slice_bitcast_fusion.18), channel_id=1, source_target_pairs={{0,8},{8,16},{16,24},{24,32},{32,40},{40,48},{48,56},{56,64},{64,7... | collective-permute-start | bytes 1544 | tf_op jit(solution)/shard_map/ppermute | solution.py:16
  351.1 18.1 %all-to-all-start.1 = ((f32[8,1,64,128]{3,2,1,0:T(8,128)}), f32[8,1,64,128]{3,2,1,0:T(8,128)S(1)}, u32[]{:S(2)}, u32[]{:S(2)}) async-start(f32[8,1,64,128]{3,2,1,0:T(8,128)} %stack.13), calls=%async_computation.3 | async-start | bytes 524288 | tf_op jit(solution)/shard_map/all_to_all | solution.py:115
  357.9 208.0 %reduce-scatter.9.cloned.1.call-start = ((), (), s32[]{:S(2)}) async-start(), calls=%async_computation.10 | async-start | bytes 294912 | tf_op jit(solution)/shard_map/reduce_scatter | solution.py:87
  365.8 4.1 copy-start.10
  371.0 10.9 %copy-start.7 = (f32[64,25,128]{2,0,1:T(8,128)}, f32[64,25,128]{2,0,1:T(8,128)S(1)}, u32[]{:S(2)}) copy-start(f32[64,25,128]{2,0,1:T(8,128)S(1)} %get-tuple-element.275) | copy-start | bytes 2457604
  531.8 10.3 %collective-permute-start.4 = (f32[128]{0:T(128)S(1)}, f32[128]{0:T(128)S(1)}, u32[]{:S(2)}, u32[]{:S(2)}) collective-permute-start(f32[128]{0:T(128)S(1)} %slice_bitcast_fusion.17), channel_id=1, source_target_pairs={{8,0},{16,8},{24,16},{32,24},{40,32},{48,40},{56,48},{64,56},{72,6... | collective-permute-start | bytes 1544 | tf_op jit(solution)/shard_map/ppermute | solution.py:16
  538.5 28.8 %copy-start.4 = (f32[64,25,128]{2,0,1:T(8,128)S(1)}, f32[64,25,128]{2,0,1:T(8,128)}, u32[]{:S(2)}) copy-start(f32[64,25,128]{2,0,1:T(8,128)} %copy-done.3) | copy-start | bytes 2457604
  571.7 22.5 %collective-permute-start.5 = (f32[128]{0:T(128)S(1)}, f32[128]{0:T(128)S(1)}, u32[]{:S(2)}, u32[]{:S(2)}) collective-permute-start(f32[128]{0:T(128)S(1)} %slice_bitcast_fusion.16), channel_id=1, source_target_pairs={{0,8},{8,16},{16,24},{24,32},{32,40},{40,48},{48,56},{56,64},{64,7... | collective-permute-start | bytes 1544 | tf_op jit(solution)/shard_map/ppermute | solution.py:16
  575.2 20.3 %all-to-all-start.2 = ((f32[8,1,64,128]{3,2,1,0:T(8,128)}), f32[8,1,64,128]{3,2,1,0:T(8,128)S(1)}, u32[]{:S(2)}, u32[]{:S(2)}) async-start(f32[8,1,64,128]{3,2,1,0:T(8,128)} %stack.14), calls=%async_computation.5 | async-start | bytes 524288 | tf_op jit(solution)/shard_map/all_to_all | solution.py:115
  582.0 214.1 %reduce-scatter.11.cloned.1.call-start = ((), (), s32[]{:S(2)}) async-start(), calls=%async_computation.11 | async-start | bytes 294912 | tf_op jit(solution)/shard_map/reduce_scatter | solution.py:87
  589.9 9.1 %copy-start.8 = (f32[64,25,128]{2,0,1:T(8,128)S(1)}, f32[64,25,128]{2,0,1:T(8,128)}, u32[]{:S(2)}) copy-start(f32[64,25,128]{2,0,1:T(8,128)} %copy-done.7) | copy-start | bytes 2457604
  601.1 10.9 %copy-start.5 = (f32[64,25,128]{2,0,1:T(8,128)}, f32[64,25,128]{2,0,1:T(8,128)S(1)}, u32[]{:S(2)}) copy-start(f32[64,25,128]{2,0,1:T(8,128)S(1)} %get-tuple-element.271) | copy-start | bytes 2457604
  761.9 10.2 %collective-permute-start.6 = (f32[128]{0:T(128)S(1)}, f32[128]{0:T(128)S(1)}, u32[]{:S(2)}, u32[]{:S(2)}) collective-permute-start(f32[128]{0:T(128)S(1)} %slice_bitcast_fusion.15), channel_id=1, source_target_pairs={{8,0},{16,8},{24,16},{32,24},{40,32},{48,40},{56,48},{64,56},{72,6... | collective-permute-start | bytes 1544 | tf_op jit(solution)/shard_map/ppermute | solution.py:16
  802.3 22.6 %collective-permute-start.7 = (f32[128]{0:T(128)S(1)}, f32[128]{0:T(128)S(1)}, u32[]{:S(2)}, u32[]{:S(2)}) collective-permute-start(f32[128]{0:T(128)S(1)} %slice_bitcast_fusion.14), channel_id=1, source_target_pairs={{0,8},{8,16},{16,24},{24,32},{32,40},{40,48},{48,56},{56,64},{64,7... | collective-permute-start | bytes 1544 | tf_op jit(solution)/shard_map/ppermute | solution.py:16
  805.8 19.0 %all-to-all-start.3 = ((f32[8,1,64,128]{3,2,1,0:T(8,128)}), f32[8,1,64,128]{3,2,1,0:T(8,128)S(1)}, u32[]{:S(2)}, u32[]{:S(2)}) async-start(f32[8,1,64,128]{3,2,1,0:T(8,128)} %stack.15), calls=%async_computation.7 | async-start | bytes 524288 | tf_op jit(solution)/shard_map/all_to_all | solution.py:115
  812.5 8.0 copy-start.11
  822.7 2.8 copy-start.6
  825.6 2.4 copy-start.1
  (2 other events, 1.9 us)
Sparse Core Ops, SparseCore 0:
  12.1 36.2 reduce-scatter.4
  309.7 31.2 reduce-scatter.6
  534.6 31.2 reduce-scatter.8
  764.8 31.2 reduce-scatter.10
